TPU v7x, 256 devices: a whole 4x4x8 slice. The times are simulated.
256 devices in a mesh: cluster: 16 (over x, y), sub: 16 (over z, core).
Axes of the slice: x: 4, y: 4, z: 8, core: 2. Of those that a mesh axis runs over, the one named last changes fastest.
Arguments:
- dual_ops: float32 [16, 16, 1408, 1408], P('cluster', 'sub'), may hold values from -1 to 4.5, as said below
- contributions: float32 [16, 16, 1408, 64], P('cluster', 'sub'), may hold values from -6 to 6
- block_sizes: int32 [16, 16, 4], P('cluster', 'sub'), may hold values from 0 to 352, as said below
- mult_map: int32 [16, 16, 1408], P('cluster', 'sub'), may hold values from 0 to 1407, each once within a row
- coarse_basis: float32 [16, 16, 32, 704], P('cluster', 'sub'), may hold values from -0.21875 to 0.21875
- coarse_inverse: float32 [16, 512, 512], P('cluster'), may hold values from -0.1 to 0.5, as said below
Outputs:
- solution: float32 [16, 16, 1408, 64], P('cluster', 'sub')
- residual: float32 [16, 16, 1408, 64], P('cluster', 'sub')
Inputs may be any that keep to these rules, and one draw needn't show every extreme that they name: `dual_ops`: symmetric positive definite for each subdomain. block_sizes[c, s, k] equals the count on the facing side of the neighbour across side k; sides at the ends of an axis hold 0, all others 352 // 4 to 352; some side holds exactly 352. `mult_map`: for each subdomain a permutation of the 1408 slots. `coarse_inverse`: symmetric for each cluster.
All inputs are finite; a program needn't handle non-finite values.
Results may differ from a plain program's by a relative error of at most 0.0003.
Values sent between devices are 32-bit elements; how exact they have to be, the bound alone decides.
A program may use at most 64 MiB of HBM per device.

v0:
```python
import jax
import jax.numpy as jnp
from jax import lax
from jax.sharding import PartitionSpec as P

ITERS = 2
precise = lax.Precision.HIGHEST


def extended(value, sides, width):
    for axis, dim in sides:
        peers, length = (lax.axis_size(axis), value.shape[dim])
        up = [(i, (i + 1) % peers) for i in range(peers - 1)]
        down = [(j, i) for i, j in up]
        last = lax.slice_in_dim(value, length - width, length, axis=dim)
        leading = lax.slice_in_dim(value, 0, width, axis=dim)
        before = lax.ppermute(last, axis, up)
        after = lax.ppermute(leading, axis, down)
        value = jnp.concatenate([before, value, after], axis=dim)
    return value


def products(left, right):
    return lax.dot_general(
        left, right, (((0,), (0,)), ((), ())), precision=precise, preferred_element_type=jnp.float32
    )


def matmul(left, right):
    return jnp.dot(left, right, precision=precise, preferred_element_type=jnp.float32)


def chol_solve(factor, target):
    middle = lax.linalg.triangular_solve(factor, target, left_side=True, lower=True)
    return lax.linalg.triangular_solve(factor, middle, left_side=True, lower=True, transpose_a=True)


def join_pair(side_pair, padded):
    return jnp.stack([side_pair[0] + padded[0], side_pair[1] + padded[3]])


def shards(dual_ops, contributions, block_sizes, mult_map, coarse_basis, coarse_inverse):
    operator = dual_ops[0, 0]
    local_rhs = contributions[0, 0]
    side_sizes = block_sizes[0, 0]
    slot_map = mult_map[0, 0]
    basis_rows = coarse_basis[0, 0]
    coarse_matrix = coarse_inverse[0]
    orders = operator.shape[0]
    face_rows = orders // 4
    mode_count = basis_rows.shape[0]
    columns = local_rhs.shape[1]
    row_index = jnp.arange(orders, dtype=jnp.int32)
    row_side = row_index // face_rows
    row_place = row_index % face_rows
    side_match = row_side[:, None] == jnp.arange(4, dtype=jnp.int32)[None, :]
    row_limit = jnp.sum(jnp.where(side_match, side_sizes[None, :], 0), axis=1)
    live_rows = (row_place < row_limit).astype(jnp.float32)[:, None]
    row_weight = live_rows * jnp.where(row_side % 2 == 0, -1.0, 1.0).astype(jnp.float32)[:, None]
    inverse_map = jnp.argsort(slot_map)
    position = lax.axis_index("sub")
    lower_zeros = jnp.zeros((2 * face_rows, columns), jnp.float32)

    def assemble(values):
        blocks = (values * row_weight).reshape(4, face_rows, columns)
        along_sub = blocks[0:2]
        along_cluster = blocks[2:4]
        sub_halo = extended(along_sub, (("sub", 0),), 1)
        cluster_halo = extended(along_cluster, (("cluster", 0),), 1)
        joined = jnp.concatenate(
            [join_pair(along_sub, sub_halo), join_pair(along_cluster, cluster_halo)], axis=0
        )
        return joined.reshape(orders, columns) * live_rows

    selected = lax.dynamic_slice_in_dim(coarse_matrix, position * mode_count, mode_count, 0)

    def accumulate(piece_rows):
        return matmul(selected, piece_rows)

    def project(values):
        signed = (values * row_weight)[: 2 * face_rows]
        moments = matmul(basis_rows, signed)
        coefficients = accumulate(lax.all_gather(moments, "sub", axis=0, tiled=True))
        lifted = products(basis_rows, coefficients) * row_weight[: 2 * face_rows]
        side_pair = lifted.reshape(2, face_rows, columns)
        coarse_halo = extended(side_pair, (("sub", 0),), 1)
        upper = join_pair(side_pair, coarse_halo).reshape(2 * face_rows, columns)
        correction = jnp.concatenate([upper, lower_zeros], axis=0) * live_rows
        return values - correction

    residual = project(assemble(local_rhs))
    solution = jnp.zeros_like(residual)
    direction = residual
    for iteration in range(ITERS):
        local_vals = jnp.take(project(direction) * row_weight, slot_map, axis=0)
        mapped = matmul(operator, local_vals)
        mapped = project(assemble(jnp.take(mapped, inverse_map, axis=0)))
        curvature, descent = lax.psum(
            (0.5 * products(direction, mapped), 0.5 * products(direction, residual)),
            ("cluster", "sub"),
        )
        factor = jnp.linalg.cholesky(curvature)
        step_size = chol_solve(factor, descent)
        solution = solution + matmul(direction, step_size)
        residual = residual - matmul(mapped, step_size)
        if iteration + 1 < ITERS:
            coupling = lax.psum(0.5 * products(mapped, residual), ("cluster", "sub"))
            direction_mix = -chol_solve(factor, coupling)
            direction = residual + matmul(direction, direction_mix)
    return (solution[None, None], residual[None, None])


def solution(mesh):
    return jax.shard_map(
        shards,
        mesh=mesh,
        in_specs=(
            P("cluster", "sub", None, None),
            P("cluster", "sub", None, None),
            P("cluster", "sub", None),
            P("cluster", "sub", None),
            P("cluster", "sub", None, None),
            P("cluster", None, None),
        ),
        out_specs=(P("cluster", "sub", None, None), P("cluster", "sub", None, None)),
        check_vma=False,
    )
```

profile of v0, /device:TPU:1, one launch (start us, length us, event | category | flops | bytes accessed | tf_op | source)
XLA Modules:
  0.0 490.3 jit_solution(13150986672781962935)
XLA Ops:
  2.7 4.9 %collective-permute-start = (f32[1,352,64]{1,2,0:T(8,128)S(1)}, f32[1,352,64]{1,2,0:T(8,128)S(1)}, u32[]{:S(2)}, u32[]{:S(2)}) collective-permute-start(f32[1,352,64]{1,2,0:T(8,128)S(1)} %get-tuple-element.34), channel_id=1, source_target_pairs={{0,1},{1,2},{2,3},{3,4},{4,5},{5,6},{6,7},{7,8},{8,9},{9,10},{10,1... | collective-permute-start | bytes 270344 | tf_op jit(solution)/shard_map/ppermute | solution.py:17
  7.6 3.2 collective-permute-start.2
  10.9 1.3 collective-permute-start.3
  12.2 1.9 collective-permute-start.1
  14.9 5.0 %sort.17 = (s32[1408]{0:T(1024)}, s32[1408]{0:T(1024)S(1)}) sort(s32[1408]{0:T(1024)S(1)} %reduce.5, s32[1408]{0:T(1024)S(1)} %iota.76), dimensions={0}, to_apply=%region_1.3 | sort | flops 15488 | bytes 22528 | tf_op jit(solution)/shard_map/jit(argsort)/sort | solution.py:60
  22.0 20.7 %all_gather.15 = f32[512,64]{1,0:T(8,128)S(1)} all-gather(f32[32,64]{1,0:T(8,128)S(1)} %convolution_bitcast_fusion.4), channel_id=1, replica_groups=mesh['cluster'=16,'sub'=16] {'sub'}, dimensions={0}, use_global_device_ids=true | all-gather | bytes 139264 | tf_op jit(solution)/shard_map/all_gather | solution.py:83
  44.3 1.9 collective-permute-start.4
  46.2 2.4 collective-permute-start.5
  48.7 3.5 collective-permute-done.5
  53.0 15.7 %all_gather.16 = f32[512,64]{1,0:T(8,128)S(1)} all-gather(f32[32,64]{1,0:T(8,128)S(1)} %convolution_bitcast_fusion.3), channel_id=1, replica_groups=mesh['cluster'=16,'sub'=16] {'sub'}, dimensions={0}, use_global_device_ids=true | all-gather | bytes 139264 | tf_op jit(solution)/shard_map/all_gather | solution.py:83
  69.4 1.9 collective-permute-start.6
  71.4 2.4 collective-permute-start.7
  73.8 3.5 collective-permute-done.7
  78.1 2.7 gather_fusion
  80.8 10.9 %fusion.6 = f32[1408,64]{0,1:T(8,128)S(1)} fusion(f32[1,1,1408,1408]{3,2,1,0:T(8,128)} %param.13, f32[1408,64]{1,0:T(8,128)S(1)} %gather_fusion, pred[1408]{0:T(1024)(128)(4,1)S(1)} %compare_and_fusion.1), kind=kOutput, calls=%fused_computation.14 | convolution fusion | flops 1522622464 | bytes 8652160 | tf_op jit(solution)/shard_map/dot_general | solution.py:30
  91.9 2.7 gather_fusion.1
  95.1 1.9 collective-permute-start.8
  97.0 4.0 collective-permute-start.10
  102.3 2.7 collective-permute-start.9
  105.0 1.3 collective-permute-done.11
  106.3 1.9 collective-permute-done.9
  109.2 18.1 %all_gather.17 = f32[512,64]{1,0:T(8,128)S(1)} all-gather(f32[32,64]{1,0:T(8,128)S(1)} %convolution_bitcast_fusion.2), channel_id=1, replica_groups=mesh['cluster'=16,'sub'=16] {'sub'}, dimensions={0}, use_global_device_ids=true | all-gather | bytes 139264 | tf_op jit(solution)/shard_map/all_gather | solution.py:83
  128.0 2.2 collective-permute-start.12
  130.2 2.3 collective-permute-start.13
  133.0 3.1 collective-permute-done.13
  137.1 82.8 %all-reduce.6 = (f32[64,64]{0,1:T(8,128)S(1)}, f32[64,64]{0,1:T(8,128)S(1)}) all-reduce(f32[64,64]{0,1:T(8,128)S(1)} %convolution_multiply_fusion.8, f32[64,64]{0,1:T(8,128)S(1)} %convolution_multiply_fusion.9), channel_id=1, replica_groups=mesh['cluster'=16,'sub'=16] {'cluster','sub'}, use_global_device_ids=true, to_apply=%region_5.8 | all-reduce | flops 8192 | bytes 65536 | tf_op jit(solution)/shard_map/psum | solution.py:98
  220.0 5.8 %cholesky.44 = f32[64,64]{1,0:T(8,128)S(1)} custom-call(f32[64,64]{1,0:T(8,128)S(1)} %fusion.69), custom_call_target="Cholesky" | custom-call | tf_op jit(solution)/shard_map/jit(cholesky)/cholesky | solution.py:102
  227.2 4.9 custom-call.13
  233.5 72.9 %psum.37 = f32[64,64]{0,1:T(8,128)S(1)} all-reduce(f32[64,64]{0,1:T(8,128)S(1)} %convolution_multiply_fusion.7), channel_id=1, replica_groups=mesh['cluster'=16,'sub'=16] {'cluster','sub'}, use_global_device_ids=true, to_apply=%region_6.11 | all-reduce | flops 4096 | bytes 32768 | tf_op jit(solution)/shard_map/psum | solution.py:107
  307.6 17.4 %all_gather.18 = f32[512,64]{1,0:T(8,128)S(1)} all-gather(f32[32,64]{1,0:T(8,128)S(1)} %convolution_bitcast_fusion.1), channel_id=1, replica_groups=mesh['cluster'=16,'sub'=16] {'sub'}, dimensions={0}, use_global_device_ids=true | all-gather | bytes 139264 | tf_op jit(solution)/shard_map/all_gather | solution.py:83
  325.8 1.9 collective-permute-start.14
  327.7 2.6 collective-permute-start.15
  330.3 3.3 collective-permute-done.15
  334.4 3.6 gather_fusion.2
  338.1 11.0 %fusion.9 = f32[1408,64]{0,1:T(8,128)S(1)} fusion(f32[1,1,1408,1408]{3,2,1,0:T(8,128)} %param.13, f32[1408,64]{1,0:T(8,128)} %gather_fusion.2, pred[1408]{0:T(1024)(128)(4,1)S(1)} %compare_and_fusion.1), kind=kOutput, calls=%fused_computation.15 | convolution fusion | flops 1522622464 | bytes 8652160 | tf_op jit(solution)/shard_map/dot_general | solution.py:30
  349.4 3.6 gather_fusion.3
  353.0 1.4 copy.75
  354.6 1.9 collective-permute-start.16
  356.5 2.9 collective-permute-start.18
  360.7 2.7 collective-permute-start.17
  364.7 1.9 collective-permute-done.17
  367.6 17.8 %all_gather.19 = f32[512,64]{1,0:T(8,128)S(1)} all-gather(f32[32,64]{1,0:T(8,128)S(1)} %convolution_bitcast_fusion), channel_id=1, replica_groups=mesh['cluster'=16,'sub'=16] {'sub'}, dimensions={0}, use_global_device_ids=true | all-gather | bytes 139264 | tf_op jit(solution)/shard_map/all_gather | solution.py:83
  386.1 2.1 collective-permute-start.20
  388.2 2.2 collective-permute-start.21
  391.0 3.2 collective-permute-done.21
  395.1 80.1 %all-reduce.5 = (f32[64,64]{0,1:T(8,128)S(1)}, f32[64,64]{0,1:T(8,128)S(1)}) all-reduce(f32[64,64]{0,1:T(8,128)S(1)} %convolution_multiply_fusion.5, f32[64,64]{0,1:T(8,128)S(1)} %convolution_multiply_fusion.6), channel_id=1, replica_groups=mesh['cluster'=16,'sub'=16] {'cluster','sub'}, use_global_device_ids=true, to_apply=%region_8.13 | all-reduce | flops 8192 | bytes 65536 | tf_op jit(solution)/shard_map/psum | solution.py:98
  475.3 5.8 %cholesky.55 = f32[64,64]{1,0:T(8,128)S(1)} custom-call(f32[64,64]{1,0:T(8,128)S(1)} %fusion.61), custom_call_target="Cholesky" | custom-call | tf_op jit(solution)/shard_map/jit(cholesky)/cholesky | solution.py:102
  482.5 4.9 custom-call.17
  (132 shorter events, 29.6 us)
Async XLA Ops:
  0.6 42.1 %copy-start = (f32[1,512,512]{2,1,0:T(8,128)S(1)}, f32[1,512,512]{2,1,0:T(8,128)}, u32[]{:S(2)}) copy-start(f32[1,512,512]{2,1,0:T(8,128)} %param.18) | copy-start | bytes 3145732
  0.6 52.0 %copy-start.1 = (f32[1,1,32,704]{3,2,1,0:T(8,128)S(1)}, f32[1,1,32,704]{3,2,1,0:T(8,128)}, u32[]{:S(2)}) copy-start(f32[1,1,32,704]{3,2,1,0:T(8,128)} %param.17) | copy-start | bytes 270340
  2.7 17.3 %collective-permute-start = (f32[1,352,64]{1,2,0:T(8,128)S(1)}, f32[1,352,64]{1,2,0:T(8,128)S(1)}, u32[]{:S(2)}, u32[]{:S(2)}) collective-permute-start(f32[1,352,64]{1,2,0:T(8,128)S(1)} %get-tuple-element.34), channel_id=1, source_target_pairs={{0,1},{1,2},{2,3},{3,4},{4,5},{5,6},{6,7},{7,8},{8,9},{9,10},{10,1... | collective-permute-start | bytes 270344 | tf_op jit(solution)/shard_map/ppermute | solution.py:17
  7.6 12.4 %collective-permute-start.2 = (f32[1,352,64]{1,2,0:T(8,128)S(1)}, f32[1,352,64]{1,2,0:T(8,128)S(1)}, u32[]{:S(2)}, u32[]{:S(2)}) collective-permute-start(f32[1,352,64]{1,2,0:T(8,128)S(1)} %get-tuple-element.35), channel_id=1, source_target_pairs={{0,16},{16,32},{32,48},{48,64},{64,80},{80,96},{96,112},{112,128},... | collective-permute-start | bytes 270344 | tf_op jit(solution)/shard_map/ppermute | solution.py:17
  10.9 9.2 %collective-permute-start.3 = (f32[1,352,64]{1,2,0:T(8,128)S(1)}, f32[1,352,64]{1,2,0:T(8,128)S(1)}, u32[]{:S(2)}, u32[]{:S(2)}) collective-permute-start(f32[1,352,64]{1,2,0:T(8,128)S(1)} %get-tuple-element.36), channel_id=1, source_target_pairs={{16,0},{32,16},{48,32},{64,48},{80,64},{96,80},{112,96},{128,112},... | collective-permute-start | bytes 270344 | tf_op jit(solution)/shard_map/ppermute | solution.py:18
  12.2 7.9 %collective-permute-start.1 = (f32[1,352,64]{1,2,0:T(8,128)S(1)}, f32[1,352,64]{1,2,0:T(8,128)S(1)}, u32[]{:S(2)}, u32[]{:S(2)}) collective-permute-start(f32[1,352,64]{1,2,0:T(8,128)S(1)} %get-tuple-element.37), channel_id=1, source_target_pairs={{1,0},{2,1},{3,2},{4,3},{5,4},{6,5},{7,6},{8,7},{9,8},{10,9},{11,1... | collective-permute-start | bytes 270344 | tf_op jit(solution)/shard_map/ppermute | solution.py:18
  44.3 4.4 collective-permute-start.4
  46.2 5.9 %collective-permute-start.5 = (f32[1,352,64]{1,2,0:T(8,128)S(1)}, f32[1,352,64]{1,2,0:T(8,128)S(1)}, u32[]{:S(2)}, u32[]{:S(2)}) collective-permute-start(f32[1,352,64]{1,2,0:T(8,128)S(1)} %get-tuple-element.57), channel_id=1, source_target_pairs={{1,0},{2,1},{3,2},{4,3},{5,4},{6,5},{7,6},{8,7},{9,8},{10,9},{11,1... | collective-permute-start | bytes 270344 | tf_op jit(solution)/shard_map/ppermute | solution.py:18
  69.4 4.4 collective-permute-start.6
  71.4 5.9 %collective-permute-start.7 = (f32[1,352,64]{1,2,0:T(8,128)S(1)}, f32[1,352,64]{1,2,0:T(8,128)S(1)}, u32[]{:S(2)}, u32[]{:S(2)}) collective-permute-start(f32[1,352,64]{1,2,0:T(8,128)S(1)} %get-tuple-element.53), channel_id=1, source_target_pairs={{1,0},{2,1},{3,2},{4,3},{5,4},{6,5},{7,6},{8,7},{9,8},{10,9},{11,1... | collective-permute-start | bytes 270344 | tf_op jit(solution)/shard_map/ppermute | solution.py:18
  95.1 9.9 %collective-permute-start.8 = (f32[1,352,64]{1,2,0:T(8,128)S(1)}, f32[1,352,64]{1,2,0:T(8,128)S(1)}, u32[]{:S(2)}, u32[]{:S(2)}) collective-permute-start(f32[1,352,64]{1,2,0:T(8,128)S(1)} %get-tuple-element.26), channel_id=1, source_target_pairs={{0,1},{1,2},{2,3},{3,4},{4,5},{5,6},{6,7},{7,8},{8,9},{9,10},{10,1... | collective-permute-start | bytes 270344 | tf_op jit(solution)/shard_map/ppermute | solution.py:17
  97.0 8.0 %collective-permute-start.10 = (f32[1,352,64]{1,2,0:T(8,128)S(1)}, f32[1,352,64]{1,2,0:T(8,128)S(1)}, u32[]{:S(2)}, u32[]{:S(2)}) collective-permute-start(f32[1,352,64]{1,2,0:T(8,128)S(1)} %get-tuple-element.27), channel_id=1, source_target_pairs={{0,16},{16,32},{32,48},{48,64},{64,80},{80,96},{96,112},{112,128},... | collective-permute-start | bytes 270344 | tf_op jit(solution)/shard_map/ppermute | solution.py:17
  101.0 5.4 %collective-permute-start.11 = (f32[1,352,64]{1,2,0:T(8,128)S(1)}, f32[1,352,64]{1,2,0:T(8,128)S(1)}, u32[]{:S(2)}, u32[]{:S(2)}) collective-permute-start(f32[1,352,64]{1,2,0:T(8,128)S(1)} %get-tuple-element.28), channel_id=1, source_target_pairs={{16,0},{32,16},{48,32},{64,48},{80,64},{96,80},{112,96},{128,112},... | collective-permute-start | bytes 270344 | tf_op jit(solution)/shard_map/ppermute | solution.py:18
  102.3 5.9 %collective-permute-start.9 = (f32[1,352,64]{1,2,0:T(8,128)S(1)}, f32[1,352,64]{1,2,0:T(8,128)S(1)}, u32[]{:S(2)}, u32[]{:S(2)}) collective-permute-start(f32[1,352,64]{1,2,0:T(8,128)S(1)} %get-tuple-element.29), channel_id=1, source_target_pairs={{1,0},{2,1},{3,2},{4,3},{5,4},{6,5},{7,6},{8,7},{9,8},{10,9},{11,1... | collective-permute-start | bytes 270344 | tf_op jit(solution)/shard_map/ppermute | solution.py:18
  128.0 5.0 %collective-permute-start.12 = (f32[1,352,64]{1,2,0:T(8,128)S(1)}, f32[1,352,64]{1,2,0:T(8,128)S(1)}, u32[]{:S(2)}, u32[]{:S(2)}) collective-permute-start(f32[1,352,64]{1,2,0:T(8,128)S(1)} %get-tuple-element.48), channel_id=1, source_target_pairs={{0,1},{1,2},{2,3},{3,4},{4,5},{5,6},{6,7},{7,8},{8,9},{9,10},{10,1... | collective-permute-start | bytes 270344 | tf_op jit(solution)/shard_map/ppermute | solution.py:17
  130.2 5.9 %collective-permute-start.13 = (f32[1,352,64]{1,2,0:T(8,128)S(1)}, f32[1,352,64]{1,2,0:T(8,128)S(1)}, u32[]{:S(2)}, u32[]{:S(2)}) collective-permute-start(f32[1,352,64]{1,2,0:T(8,128)S(1)} %get-tuple-element.49), channel_id=1, source_target_pairs={{1,0},{2,1},{3,2},{4,3},{5,4},{6,5},{7,6},{8,7},{9,8},{10,9},{11,1... | collective-permute-start | bytes 270344 | tf_op jit(solution)/shard_map/ppermute | solution.py:18
  325.8 4.6 collective-permute-start.14
  327.7 5.9 %collective-permute-start.15 = (f32[1,352,64]{1,2,0:T(8,128)S(1)}, f32[1,352,64]{1,2,0:T(8,128)S(1)}, u32[]{:S(2)}, u32[]{:S(2)}) collective-permute-start(f32[1,352,64]{1,2,0:T(8,128)S(1)} %get-tuple-element.45), channel_id=1, source_target_pairs={{1,0},{2,1},{3,2},{4,3},{5,4},{6,5},{7,6},{8,7},{9,8},{10,9},{11,1... | collective-permute-start | bytes 270344 | tf_op jit(solution)/shard_map/ppermute | solution.py:18
  354.6 9.3 %collective-permute-start.16 = (f32[1,352,64]{1,2,0:T(8,128)S(1)}, f32[1,352,64]{1,2,0:T(8,128)S(1)}, u32[]{:S(2)}, u32[]{:S(2)}) collective-permute-start(f32[1,352,64]{1,2,0:T(8,128)S(1)} %get-tuple-element.18), channel_id=1, source_target_pairs={{0,1},{1,2},{2,3},{3,4},{4,5},{5,6},{6,7},{7,8},{8,9},{9,10},{10,1... | collective-permute-start | bytes 270344 | tf_op jit(solution)/shard_map/ppermute | solution.py:17
  356.5 7.4 %collective-permute-start.18 = (f32[1,352,64]{1,2,0:T(8,128)S(1)}, f32[1,352,64]{1,2,0:T(8,128)S(1)}, u32[]{:S(2)}, u32[]{:S(2)}) collective-permute-start(f32[1,352,64]{1,2,0:T(8,128)S(1)} %get-tuple-element.19), channel_id=1, source_target_pairs={{0,16},{16,32},{32,48},{48,64},{64,80},{80,96},{96,112},{112,128},... | collective-permute-start | bytes 270344 | tf_op jit(solution)/shard_map/ppermute | solution.py:17
  359.4 5.4 %collective-permute-start.19 = (f32[1,352,64]{1,2,0:T(8,128)S(1)}, f32[1,352,64]{1,2,0:T(8,128)S(1)}, u32[]{:S(2)}, u32[]{:S(2)}) collective-permute-start(f32[1,352,64]{1,2,0:T(8,128)S(1)} %get-tuple-element.20), channel_id=1, source_target_pairs={{16,0},{32,16},{48,32},{64,48},{80,64},{96,80},{112,96},{128,112},... | collective-permute-start | bytes 270344 | tf_op jit(solution)/shard_map/ppermute | solution.py:18
  360.7 5.9 %collective-permute-start.17 = (f32[1,352,64]{1,2,0:T(8,128)S(1)}, f32[1,352,64]{1,2,0:T(8,128)S(1)}, u32[]{:S(2)}, u32[]{:S(2)}) collective-permute-start(f32[1,352,64]{1,2,0:T(8,128)S(1)} %get-tuple-element.21), channel_id=1, source_target_pairs={{1,0},{2,1},{3,2},{4,3},{5,4},{6,5},{7,6},{8,7},{9,8},{10,9},{11,1... | collective-permute-start | bytes 270344 | tf_op jit(solution)/shard_map/ppermute | solution.py:18
  386.1 4.8 collective-permute-start.20
  388.2 5.9 %collective-permute-start.21 = (f32[1,352,64]{1,2,0:T(8,128)S(1)}, f32[1,352,64]{1,2,0:T(8,128)S(1)}, u32[]{:S(2)}, u32[]{:S(2)}) collective-permute-start(f32[1,352,64]{1,2,0:T(8,128)S(1)} %get-tuple-element.41), channel_id=1, source_target_pairs={{1,0},{2,1},{3,2},{4,3},{5,4},{6,5},{7,6},{8,7},{9,8},{10,9},{11,1... | collective-permute-start | bytes 270344 | tf_op jit(solution)/shard_map/ppermute | solution.py:18
where the time goes:
time: 492 us; the launch traced here: 490 us
  blocking collectives  326 us (66%)
  starting transfers between devices  52 us (11%)
  matrix products  35.9 us (7%)
  other arithmetic  33.3 us (7%)
  waiting for transfers between devices  22.5 us (5%)
  local copies, waits for them, and re-layouts  19.4 us (4%)
    psum x2, blocking collectives, shards(): lax.psum((0.5 * products(direction, mapped), 0.5 * products(direction, re...  163 us
    all_gather x5, blocking collectives, project(): lax.all_gather(moments, 'sub', axis=0, tiled=True)  89.7 us
    psum x1, blocking collectives, shards(): coupling = lax.psum(0.5 * products(mapped, residual), ('cluster', 'sub'))  72.9 us
    dot_general x17, matrix products, matmul(): jnp.dot(left, right, precision=precise, preferred_element_type=jnp.float32)  29.5 us
    ppermute x11, starting transfers between devices, extended(): before = lax.ppermute(last, axis, up)  28.8 us
    ppermute x11, starting transfers between devices, extended(): after = lax.ppermute(leading, axis, down)  23.2 us
    ppermute x11, waiting for transfers between devices, extended(): after = lax.ppermute(leading, axis, down)  22.5 us
    another operation x6, other arithmetic, shards(): factor = jnp.linalg.cholesky(curvature)  13 us
  transfers between devices with their start and end apart: 22, of which 9 were waited for; matrix products, arithmetic and copies ran while one was open for 1% of the time, Pallas kernels for 0%

commit v1 on v0

--- a/solution.py
+++ b/solution.py
@@ -95,9 +95,9 @@
         local_vals = jnp.take(project(direction) * row_weight, slot_map, axis=0)
         mapped = matmul(operator, local_vals)
         mapped = project(assemble(jnp.take(mapped, inverse_map, axis=0)))
-        curvature, descent = lax.psum(
-            (0.5 * products(direction, mapped), 0.5 * products(direction, residual)),
-            ("cluster", "sub"),
+        modes_store = lambda s0: lax.psum(lax.psum(s0, "cluster"), axis_name="sub")
+        curvature, descent = modes_store(
+            (0.5 * products(direction, mapped), 0.5 * products(direction, residual))
         )
         factor = jnp.linalg.cholesky(curvature)
         step_size = chol_solve(factor, descent)

time: 492 us -> 564 us (1.15)
  blocking collectives: 326 us -> 396 us
    psum x2 -> x4, blocking collectives: 163 us -> 229 us  [shards(): modes_store = lambda s0: lax.psum(lax.psum(s0, 'cluster'), axis_name='sub')]
where the time goes in v1:
time: 564 us; the launch traced here: 561 us
  blocking collectives  396 us (70%)
  starting transfers between devices  52.3 us (9%)
  matrix products  35.9 us (6%)
  other arithmetic  33.3 us (6%)
  waiting for transfers between devices  22.6 us (4%)
  local copies, waits for them, and re-layouts  19.4 us (3%)
    psum x4, blocking collectives, shards(): modes_store = lambda s0: lax.psum(lax.psum(s0, 'cluster'), axis_name='sub')  229 us
    all_gather x5, blocking collectives, project(): lax.all_gather(moments, 'sub', axis=0, tiled=True)  89.4 us
    psum x1, blocking collectives, shards(): coupling = lax.psum(0.5 * products(mapped, residual), ('cluster', 'sub'))  77.3 us
    dot_general x17, matrix products, matmul(): jnp.dot(left, right, precision=precise, preferred_element_type=jnp.float32)  29.5 us
    ppermute x11, starting transfers between devices, extended(): before = lax.ppermute(last, axis, up)  29.2 us
    ppermute x11, starting transfers between devices, extended(): after = lax.ppermute(leading, axis, down)  23.2 us
    ppermute x11, waiting for transfers between devices, extended(): after = lax.ppermute(leading, axis, down)  22.6 us
    another operation x6, other arithmetic, shards(): factor = jnp.linalg.cholesky(curvature)  13 us
  transfers between devices with their start and end apart: 22, of which 9 were waited for; matrix products, arithmetic and copies ran while one was open for 1% of the time, Pallas kernels for 0%

profile of v1, /device:TPU:1, one launch (start us, length us, event | category | flops | bytes accessed | tf_op | source)
XLA Modules:
  0.0 561.2 jit_solution(9594386711244053501)
XLA Ops:
  2.7 4.9 collective-permute-start
  7.6 3.2 collective-permute-start.2
  12.2 1.9 collective-permute-start.1
  14.9 5.0 sort.17
  22.0 20.7 %all_gather.15 = f32[512,64]{1,0:T(8,128)S(1)} all-gather(f32[32,64]{1,0:T(8,128)S(1)} %convolution_bitcast_fusion.4), channel_id=1, replica_groups=mesh['cluster'=16,'sub'=16] {'sub'}, dimensions={0}, use_global_device_ids=true | all-gather | bytes 139264 | tf_op jit(solution)/shard_map/all_gather | solution.py:83
  44.3 1.9 collective-permute-start.4
  46.2 2.4 collective-permute-start.5
  48.7 3.5 collective-permute-done.5
  53.0 15.7 %all_gather.16 = f32[512,64]{1,0:T(8,128)S(1)} all-gather(f32[32,64]{1,0:T(8,128)S(1)} %convolution_bitcast_fusion.3), channel_id=1, replica_groups=mesh['cluster'=16,'sub'=16] {'sub'}, dimensions={0}, use_global_device_ids=true | all-gather | bytes 139264 | tf_op jit(solution)/shard_map/all_gather | solution.py:83
  69.4 1.9 collective-permute-start.6
  71.4 2.4 collective-permute-start.7
  73.8 3.5 collective-permute-done.7
  78.1 2.7 gather_fusion
  80.8 10.9 %fusion.6 = f32[1408,64]{0,1:T(8,128)S(1)} fusion(f32[1,1,1408,1408]{3,2,1,0:T(8,128)} %param.13, f32[1408,64]{1,0:T(8,128)S(1)} %gather_fusion, pred[1408]{0:T(1024)(128)(4,1)S(1)} %compare_and_fusion.1), kind=kOutput, calls=%fused_computation.14 | convolution fusion | flops 1522622464 | bytes 8652160 | tf_op jit(solution)/shard_map/dot_general | solution.py:30
  91.9 2.7 gather_fusion.1
  95.1 1.9 collective-permute-start.8
  97.0 4.0 collective-permute-start.10
  102.3 2.7 collective-permute-start.9
  106.3 1.9 collective-permute-done.9
  109.2 18.1 %all_gather.17 = f32[512,64]{1,0:T(8,128)S(1)} all-gather(f32[32,64]{1,0:T(8,128)S(1)} %convolution_bitcast_fusion.2), channel_id=1, replica_groups=mesh['cluster'=16,'sub'=16] {'sub'}, dimensions={0}, use_global_device_ids=true | all-gather | bytes 139264 | tf_op jit(solution)/shard_map/all_gather | solution.py:83
  128.0 2.2 collective-permute-start.12
  130.2 2.3 collective-permute-start.13
  133.0 3.1 collective-permute-done.13
  137.1 61.3 %all-reduce.8 = (f32[64,64]{0,1:T(8,128)S(1)}, f32[64,64]{0,1:T(8,128)S(1)}) all-reduce(f32[64,64]{0,1:T(8,128)S(1)} %convolution_multiply_fusion.8, f32[64,64]{0,1:T(8,128)S(1)} %convolution_multiply_fusion.9), channel_id=1, replica_groups=mesh['cluster'=16,'sub'=16] {'cluster'}, use_global_device_ids=true, to_apply=%region_6.9 | all-reduce | flops 8192 | bytes 65536 | tf_op jit(solution)/shard_map/psum | solution.py:98
  198.4 55.0 %all-reduce.6 = (f32[64,64]{0,1:T(8,128)S(1)}, f32[64,64]{0,1:T(8,128)S(1)}) all-reduce(f32[64,64]{0,1:T(8,128)S(1)} %get-tuple-element.14, f32[64,64]{0,1:T(8,128)S(1)} %get-tuple-element.15), channel_id=1, replica_groups=mesh['cluster'=16,'sub'=16] {'sub'}, use_global_device_ids=true, to_apply=%region_7.10 | all-reduce | flops 8192 | bytes 65536 | tf_op jit(solution)/shard_map/psum | solution.py:98
  253.5 5.8 %cholesky.44 = f32[64,64]{1,0:T(8,128)S(1)} custom-call(f32[64,64]{1,0:T(8,128)S(1)} %fusion.69), custom_call_target="Cholesky" | custom-call | tf_op jit(solution)/shard_map/jit(cholesky)/cholesky | solution.py:102
  260.7 4.9 custom-call.13
  267.0 77.3 %psum.67 = f32[64,64]{0,1:T(8,128)S(1)} all-reduce(f32[64,64]{0,1:T(8,128)S(1)} %convolution_multiply_fusion.7), channel_id=1, replica_groups=mesh['cluster'=16,'sub'=16] {'cluster','sub'}, use_global_device_ids=true, to_apply=%region_8.13 | all-reduce | flops 4096 | bytes 32768 | tf_op jit(solution)/shard_map/psum | solution.py:107
  345.6 17.1 %all_gather.18 = f32[512,64]{1,0:T(8,128)S(1)} all-gather(f32[32,64]{1,0:T(8,128)S(1)} %convolution_bitcast_fusion.1), channel_id=1, replica_groups=mesh['cluster'=16,'sub'=16] {'sub'}, dimensions={0}, use_global_device_ids=true | all-gather | bytes 139264 | tf_op jit(solution)/shard_map/all_gather | solution.py:83
  363.4 2.0 collective-permute-start.14
  365.3 2.6 collective-permute-start.15
  367.9 3.3 collective-permute-done.15
  372.0 3.7 gather_fusion.2
  375.7 11.0 %fusion.9 = f32[1408,64]{0,1:T(8,128)S(1)} fusion(f32[1,1,1408,1408]{3,2,1,0:T(8,128)} %param.13, f32[1408,64]{1,0:T(8,128)} %gather_fusion.2, pred[1408]{0:T(1024)(128)(4,1)S(1)} %compare_and_fusion.1), kind=kOutput, calls=%fused_computation.15 | convolution fusion | flops 1522622464 | bytes 8652160 | tf_op jit(solution)/shard_map/dot_general | solution.py:30
  387.0 3.7 gather_fusion.3
  390.7 1.4 copy.75
  392.2 1.9 collective-permute-start.16
  394.2 3.2 collective-permute-start.18
  398.6 2.7 collective-permute-start.17
  402.7 1.9 collective-permute-done.17
  405.6 17.8 %all_gather.19 = f32[512,64]{1,0:T(8,128)S(1)} all-gather(f32[32,64]{1,0:T(8,128)S(1)} %convolution_bitcast_fusion), channel_id=1, replica_groups=mesh['cluster'=16,'sub'=16] {'sub'}, dimensions={0}, use_global_device_ids=true | all-gather | bytes 139264 | tf_op jit(solution)/shard_map/all_gather | solution.py:83
  424.1 2.1 collective-permute-start.20
  426.2 2.2 collective-permute-start.21
  428.9 3.2 collective-permute-done.21
  433.1 58.5 %all-reduce.7 = (f32[64,64]{0,1:T(8,128)S(1)}, f32[64,64]{0,1:T(8,128)S(1)}) all-reduce(f32[64,64]{0,1:T(8,128)S(1)} %convolution_multiply_fusion.5, f32[64,64]{0,1:T(8,128)S(1)} %convolution_multiply_fusion.6), channel_id=1, replica_groups=mesh['cluster'=16,'sub'=16] {'cluster'}, use_global_device_ids=true, to_apply=%region_11.16 | all-reduce | flops 8192 | bytes 65536 | tf_op jit(solution)/shard_map/psum | solution.py:98
  491.5 54.6 %all-reduce.5 = (f32[64,64]{0,1:T(8,128)S(1)}, f32[64,64]{0,1:T(8,128)S(1)}) all-reduce(f32[64,64]{0,1:T(8,128)S(1)} %get-tuple-element.12, f32[64,64]{0,1:T(8,128)S(1)} %get-tuple-element.13), channel_id=1, replica_groups=mesh['cluster'=16,'sub'=16] {'sub'}, use_global_device_ids=true, to_apply=%region_12.17 | all-reduce | flops 8192 | bytes 65536 | tf_op jit(solution)/shard_map/psum | solution.py:98
  546.2 5.8 %cholesky.55 = f32[64,64]{1,0:T(8,128)S(1)} custom-call(f32[64,64]{1,0:T(8,128)S(1)} %fusion.61), custom_call_target="Cholesky" | custom-call | tf_op jit(solution)/shard_map/jit(cholesky)/cholesky | solution.py:102
  553.4 4.9 custom-call.17
  (134 shorter events, 32.2 us)
Async XLA Ops:
  0.6 42.1 %copy-start = (f32[1,512,512]{2,1,0:T(8,128)S(1)}, f32[1,512,512]{2,1,0:T(8,128)}, u32[]{:S(2)}) copy-start(f32[1,512,512]{2,1,0:T(8,128)} %param.18) | copy-start | bytes 3145732
  0.6 52.0 %copy-start.1 = (f32[1,1,32,704]{3,2,1,0:T(8,128)S(1)}, f32[1,1,32,704]{3,2,1,0:T(8,128)}, u32[]{:S(2)}) copy-start(f32[1,1,32,704]{3,2,1,0:T(8,128)} %param.17) | copy-start | bytes 270340
  2.7 17.3 %collective-permute-start = (f32[1,352,64]{1,2,0:T(8,128)S(1)}, f32[1,352,64]{1,2,0:T(8,128)S(1)}, u32[]{:S(2)}, u32[]{:S(2)}) collective-permute-start(f32[1,352,64]{1,2,0:T(8,128)S(1)} %get-tuple-element.38), channel_id=1, source_target_pairs={{0,1},{1,2},{2,3},{3,4},{4,5},{5,6},{6,7},{7,8},{8,9},{9,10},{10,1... | collective-permute-start | bytes 270344 | tf_op jit(solution)/shard_map/ppermute | solution.py:17
  7.6 12.4 %collective-permute-start.2 = (f32[1,352,64]{1,2,0:T(8,128)S(1)}, f32[1,352,64]{1,2,0:T(8,128)S(1)}, u32[]{:S(2)}, u32[]{:S(2)}) collective-permute-start(f32[1,352,64]{1,2,0:T(8,128)S(1)} %get-tuple-element.39), channel_id=1, source_target_pairs={{0,16},{16,32},{32,48},{48,64},{64,80},{80,96},{96,112},{112,128},... | collective-permute-start | bytes 270344 | tf_op jit(solution)/shard_map/ppermute | solution.py:17
  10.9 9.2 %collective-permute-start.3 = (f32[1,352,64]{1,2,0:T(8,128)S(1)}, f32[1,352,64]{1,2,0:T(8,128)S(1)}, u32[]{:S(2)}, u32[]{:S(2)}) collective-permute-start(f32[1,352,64]{1,2,0:T(8,128)S(1)} %get-tuple-element.40), channel_id=1, source_target_pairs={{16,0},{32,16},{48,32},{64,48},{80,64},{96,80},{112,96},{128,112},... | collective-permute-start | bytes 270344 | tf_op jit(solution)/shard_map/ppermute | solution.py:18
  12.2 7.9 %collective-permute-start.1 = (f32[1,352,64]{1,2,0:T(8,128)S(1)}, f32[1,352,64]{1,2,0:T(8,128)S(1)}, u32[]{:S(2)}, u32[]{:S(2)}) collective-permute-start(f32[1,352,64]{1,2,0:T(8,128)S(1)} %get-tuple-element.41), channel_id=1, source_target_pairs={{1,0},{2,1},{3,2},{4,3},{5,4},{6,5},{7,6},{8,7},{9,8},{10,9},{11,1... | collective-permute-start | bytes 270344 | tf_op jit(solution)/shard_map/ppermute | solution.py:18
  44.3 4.4 collective-permute-start.4
  46.2 5.9 %collective-permute-start.5 = (f32[1,352,64]{1,2,0:T(8,128)S(1)}, f32[1,352,64]{1,2,0:T(8,128)S(1)}, u32[]{:S(2)}, u32[]{:S(2)}) collective-permute-start(f32[1,352,64]{1,2,0:T(8,128)S(1)} %get-tuple-element.61), channel_id=1, source_target_pairs={{1,0},{2,1},{3,2},{4,3},{5,4},{6,5},{7,6},{8,7},{9,8},{10,9},{11,1... | collective-permute-start | bytes 270344 | tf_op jit(solution)/shard_map/ppermute | solution.py:18
  69.4 4.4 collective-permute-start.6
  71.4 5.9 %collective-permute-start.7 = (f32[1,352,64]{1,2,0:T(8,128)S(1)}, f32[1,352,64]{1,2,0:T(8,128)S(1)}, u32[]{:S(2)}, u32[]{:S(2)}) collective-permute-start(f32[1,352,64]{1,2,0:T(8,128)S(1)} %get-tuple-element.57), channel_id=1, source_target_pairs={{1,0},{2,1},{3,2},{4,3},{5,4},{6,5},{7,6},{8,7},{9,8},{10,9},{11,1... | collective-permute-start | bytes 270344 | tf_op jit(solution)/shard_map/ppermute | solution.py:18
  95.1 9.9 %collective-permute-start.8 = (f32[1,352,64]{1,2,0:T(8,128)S(1)}, f32[1,352,64]{1,2,0:T(8,128)S(1)}, u32[]{:S(2)}, u32[]{:S(2)}) collective-permute-start(f32[1,352,64]{1,2,0:T(8,128)S(1)} %get-tuple-element.30), channel_id=1, source_target_pairs={{0,1},{1,2},{2,3},{3,4},{4,5},{5,6},{6,7},{7,8},{8,9},{9,10},{10,1... | collective-permute-start | bytes 270344 | tf_op jit(solution)/shard_map/ppermute | solution.py:17
  97.0 8.0 %collective-permute-start.10 = (f32[1,352,64]{1,2,0:T(8,128)S(1)}, f32[1,352,64]{1,2,0:T(8,128)S(1)}, u32[]{:S(2)}, u32[]{:S(2)}) collective-permute-start(f32[1,352,64]{1,2,0:T(8,128)S(1)} %get-tuple-element.31), channel_id=1, source_target_pairs={{0,16},{16,32},{32,48},{48,64},{64,80},{80,96},{96,112},{112,128},... | collective-permute-start | bytes 270344 | tf_op jit(solution)/shard_map/ppermute | solution.py:17
  101.0 5.4 collective-permute-start.11
  102.3 5.9 %collective-permute-start.9 = (f32[1,352,64]{1,2,0:T(8,128)S(1)}, f32[1,352,64]{1,2,0:T(8,128)S(1)}, u32[]{:S(2)}, u32[]{:S(2)}) collective-permute-start(f32[1,352,64]{1,2,0:T(8,128)S(1)} %get-tuple-element.33), channel_id=1, source_target_pairs={{1,0},{2,1},{3,2},{4,3},{5,4},{6,5},{7,6},{8,7},{9,8},{10,9},{11,1... | collective-permute-start | bytes 270344 | tf_op jit(solution)/shard_map/ppermute | solution.py:18
  128.0 5.0 collective-permute-start.12
  130.2 5.9 %collective-permute-start.13 = (f32[1,352,64]{1,2,0:T(8,128)S(1)}, f32[1,352,64]{1,2,0:T(8,128)S(1)}, u32[]{:S(2)}, u32[]{:S(2)}) collective-permute-start(f32[1,352,64]{1,2,0:T(8,128)S(1)} %get-tuple-element.53), channel_id=1, source_target_pairs={{1,0},{2,1},{3,2},{4,3},{5,4},{6,5},{7,6},{8,7},{9,8},{10,9},{11,1... | collective-permute-start | bytes 270344 | tf_op jit(solution)/shard_map/ppermute | solution.py:18
  363.4 4.6 collective-permute-start.14
  365.3 5.9 %collective-permute-start.15 = (f32[1,352,64]{1,2,0:T(8,128)S(1)}, f32[1,352,64]{1,2,0:T(8,128)S(1)}, u32[]{:S(2)}, u32[]{:S(2)}) collective-permute-start(f32[1,352,64]{1,2,0:T(8,128)S(1)} %get-tuple-element.49), channel_id=1, source_target_pairs={{1,0},{2,1},{3,2},{4,3},{5,4},{6,5},{7,6},{8,7},{9,8},{10,9},{11,1... | collective-permute-start | bytes 270344 | tf_op jit(solution)/shard_map/ppermute | solution.py:18
  392.2 9.6 %collective-permute-start.16 = (f32[1,352,64]{1,2,0:T(8,128)S(1)}, f32[1,352,64]{1,2,0:T(8,128)S(1)}, u32[]{:S(2)}, u32[]{:S(2)}) collective-permute-start(f32[1,352,64]{1,2,0:T(8,128)S(1)} %get-tuple-element.22), channel_id=1, source_target_pairs={{0,1},{1,2},{2,3},{3,4},{4,5},{5,6},{6,7},{7,8},{8,9},{9,10},{10,1... | collective-permute-start | bytes 270344 | tf_op jit(solution)/shard_map/ppermute | solution.py:17
  394.2 7.7 %collective-permute-start.18 = (f32[1,352,64]{1,2,0:T(8,128)S(1)}, f32[1,352,64]{1,2,0:T(8,128)S(1)}, u32[]{:S(2)}, u32[]{:S(2)}) collective-permute-start(f32[1,352,64]{1,2,0:T(8,128)S(1)} %get-tuple-element.23), channel_id=1, source_target_pairs={{0,16},{16,32},{32,48},{48,64},{64,80},{80,96},{96,112},{112,128},... | collective-permute-start | bytes 270344 | tf_op jit(solution)/shard_map/ppermute | solution.py:17
  397.3 5.4 collective-permute-start.19
  398.6 5.9 %collective-permute-start.17 = (f32[1,352,64]{1,2,0:T(8,128)S(1)}, f32[1,352,64]{1,2,0:T(8,128)S(1)}, u32[]{:S(2)}, u32[]{:S(2)}) collective-permute-start(f32[1,352,64]{1,2,0:T(8,128)S(1)} %get-tuple-element.25), channel_id=1, source_target_pairs={{1,0},{2,1},{3,2},{4,3},{5,4},{6,5},{7,6},{8,7},{9,8},{10,9},{11,1... | collective-permute-start | bytes 270344 | tf_op jit(solution)/shard_map/ppermute | solution.py:18
  424.1 4.8 collective-permute-start.20
  426.2 5.9 %collective-permute-start.21 = (f32[1,352,64]{1,2,0:T(8,128)S(1)}, f32[1,352,64]{1,2,0:T(8,128)S(1)}, u32[]{:S(2)}, u32[]{:S(2)}) collective-permute-start(f32[1,352,64]{1,2,0:T(8,128)S(1)} %get-tuple-element.45), channel_id=1, source_target_pairs={{1,0},{2,1},{3,2},{4,3},{5,4},{6,5},{7,6},{8,7},{9,8},{10,9},{11,1... | collective-permute-start | bytes 270344 | tf_op jit(solution)/shard_map/ppermute | solution.py:18
